TPU v7x, 32 devices: a whole 2x2x4 slice. The times are simulated.
32 devices in a mesh: dp: 2 (over x), row: 4 (over y, core), col: 4 (over z).
Axes of the slice: x: 2, y: 2, z: 4, core: 2. Of those that a mesh axis runs over, the one named last changes fastest.
Arguments:
- tokens: bfloat16 [256, 4096], P(('dp', 'col'), 'row'), may hold values from -6 to 6
- up_weight: bfloat16 [4096, 8192], P('row', 'col'), may hold values from -0.09375 to 0.09375
- up_bias: float32 [8192], P('col'), may hold values from -3 to 3
- down_weight: bfloat16 [8192, 4096], P('col', 'row'), may hold values from -0.0625 to 0.0625
- out_grad: bfloat16 [256, 4096], P(('dp', 'col'), 'row'), may hold values from -6 to 6
- bucket_lengths: int32 [8], P(('dp', 'col')), may hold values from 1 to 32, as said below
Outputs:
- input_grad: bfloat16 [256, 4096], P(('dp', 'col'), 'row')
- up_weight_grad: float32 [4096, 4, 2048], P('row', 'col', 'dp')
- up_bias_grad: float32 [4, 2048], P('col', 'dp')
- down_weight_grad: float32 [4, 2048, 4096], P('col', 'dp', 'row')
Inputs may be any that keep to these rules, and one draw needn't show every extreme that they name: `bucket_lengths`: some block is full.
All inputs are finite; a program needn't handle non-finite values.
Results may differ from a plain program's by a relative error of at most 0.0055.
Values may be sent and summed in bfloat16 or wider, within the bound.
A program may use at most 128 MiB of HBM per device.

v0:
```python
import math

import jax
import jax.numpy as jnp
from jax import lax
from jax.sharding import PartitionSpec as P

coef = math.sqrt(2.0 / math.pi)


def gelu_pair(pre):
    inner = coef * (pre + 0.044715 * pre * pre * pre)
    tanh_val = jnp.tanh(inner)
    value = 0.5 * pre * (1.0 + tanh_val)
    slope = 0.5 * (1.0 + tanh_val) + 0.5 * pre * (1.0 - tanh_val * tanh_val) * coef * (
        1.0 + 3.0 * 0.044715 * pre * pre
    )
    return (value, slope)


def contract_rows(left, right):
    return lax.dot_general(
        left, right, (((0,), (0,)), ((), ())), preferred_element_type=jnp.float32
    )


def contract_cols(left, right):
    return lax.dot_general(
        left, right, (((1,), (1,)), ((), ())), preferred_element_type=jnp.float32
    )


def local(tokens, up_weight, up_bias, down_weight, out_grad, bucket_lengths):
    local_rows = out_grad.shape[0]
    blocks = bucket_lengths.shape[0]
    block_rows = local_rows // blocks
    position = jnp.arange(local_rows, dtype=jnp.int32)
    limits = jnp.repeat(bucket_lengths, block_rows, total_repeat_length=local_rows)
    live = position % block_rows < limits
    masked = jnp.where(live[:, None], out_grad, jnp.zeros_like(out_grad))
    feats, grads = (
        lax.all_gather(tokens, "col", axis=0, tiled=True),
        lax.all_gather(masked, "col", axis=0, tiled=True),
    )
    group_rows = feats.shape[0]
    down_grad = None
    share = group_rows // lax.axis_size("row")
    pre_share = lax.psum_scatter(
        jnp.dot(feats, up_weight, preferred_element_type=jnp.float32),
        "row",
        scatter_dimension=0,
        tiled=True,
    )
    value, slope = gelu_pair(pre_share + up_bias[None, :])
    act_share = value.astype(jnp.bfloat16)
    act_grad = lax.psum_scatter(
        contract_cols(
            lax.slice_in_dim(grads, 0, share * lax.axis_size("row"), axis=0), down_weight
        ),
        "row",
        scatter_dimension=0,
        tiled=True,
    )
    grad_share = (act_grad * slope).astype(jnp.bfloat16)
    act_all, grad_all = (
        lax.all_gather(act_share, "row", axis=0, tiled=True),
        lax.all_gather(grad_share, "row", axis=0, tiled=True),
    )
    up_term = contract_rows(feats, grad_all)
    bias_term = jnp.sum(grad_all.astype(jnp.float32), axis=0)[None, :]
    input_grad = lax.psum_scatter(
        contract_cols(
            lax.slice_in_dim(grad_all, 0, local_rows * lax.axis_size("col"), axis=0), up_weight
        ),
        "col",
        scatter_dimension=0,
        tiled=True,
    ).astype(jnp.bfloat16)
    up_grad, bias_grad = (
        lax.psum_scatter(up_term, "dp", scatter_dimension=1, tiled=True),
        lax.psum_scatter(bias_term, "dp", scatter_dimension=1, tiled=True),
    )
    down_grad = lax.psum_scatter(
        contract_rows(act_all, grads), "dp", scatter_dimension=0, tiled=True
    )
    narrow = up_grad.shape[1]
    return (
        input_grad,
        up_grad.reshape(up_grad.shape[0], 1, narrow),
        bias_grad.reshape(1, narrow),
        down_grad.reshape(1, narrow, down_grad.shape[1]),
    )


def solution(mesh):
    return jax.shard_map(
        local,
        mesh=mesh,
        in_specs=(
            P(("dp", "col"), "row"),
            P("row", "col"),
            P("col"),
            P("col", "row"),
            P(("dp", "col"), "row"),
            P(("dp", "col")),
        ),
        out_specs=(
            P(("dp", "col"), "row"),
            P("row", "col", "dp"),
            P("col", "dp"),
            P("col", "dp", "row"),
        ),
        check_vma=False,
    )
```

profile of v0, /device:TPU:0, one launch (start us, length us, event | category | flops | bytes accessed | tf_op | source)
XLA Modules:
  0.0 344.5 jit_solution(14165476783561700068)
XLA Ops:
  7.2 0.0 copy-start
  7.2 0.0 reduce-scatter.11.cloned.1.call-start
  7.2 15.9 %all_gather.13 = bf16[128,1024]{1,0:T(8,128)(2,1)S(1)} all-gather(bf16[32,1024]{1,0:T(8,128)(2,1)} %param.10), channel_id=1, replica_groups=mesh['dp'=2,'row'=4,'col'=4] {'col'}, dimensions={0}, use_global_device_ids=true | all-gather | bytes 327680 | tf_op jit(solution)/shard_map/all_gather | solution.py:42
  23.1 3.9 %fusion.9 = f32[128,2048]{1,0:T(8,128)} fusion(bf16[128,1024]{1,0:T(8,128)(2,1)S(1)} %all_gather.13, bf16[1024,2048]{1,0:T(8,128)(2,1)} %param.11), kind=kOutput, calls=%fused_computation.16 | convolution fusion | flops 536870912 | bytes 5505024 | tf_op jit(solution)/shard_map/dot_general | solution.py:49
  27.0 0.0 copy-start.1
  27.0 0.0 reduce-scatter.11.cloned.1.call-update
  27.0 0.0 reduce-scatter.9.cloned.1.call-start
  27.7 0.0 copy-done
  27.7 0.1 broadcast_select_fusion
  27.8 14.4 %all_gather.12 = bf16[128,1024]{1,0:T(8,128)(2,1)S(1)} all-gather(bf16[32,1024]{1,0:T(8,128)(2,1)S(1)} %broadcast_select_fusion), channel_id=1, replica_groups=mesh['dp'=2,'row'=4,'col'=4] {'col'}, dimensions={0}, use_global_device_ids=true | all-gather | bytes 327680 | tf_op jit(solution)/shard_map/all_gather | solution.py:43
  42.2 4.7 %fusion.8 = f32[128,2048]{1,0:T(8,128)} fusion(bf16[128,1024]{1,0:T(8,128)(2,1)S(1)} %all_gather.12, bf16[2048,1024]{1,0:T(8,128)(2,1)} %param.13), kind=kOutput, calls=%fused_computation.15 | convolution fusion | flops 536870912 | bytes 5505024 | tf_op jit(solution)/shard_map/dot_general | solution.py:28
  46.9 0.0 reduce-scatter.9.cloned.1.call-update
  46.9 0.0 reduce-scatter.19.cloned.1.call-start
  46.9 6.5 %reduce-scatter.11.cloned.1.call-done = f32[32,2048]{1,0:T(8,128)} async-done(((f32[128,2048]{1,0:T(8,128)}), f32[32,2048]{1,0:T(8,128)}) %reduce-scatter.11.cloned.1.call-update) | async-done | bytes 262160 | tf_op jit(solution)/shard_map/reduce_scatter | solution.py:48
  53.5 27.9 %reduce-scatter.9.cloned.1.call-done = f32[32,2048]{1,0:T(8,128)} async-done(((f32[128,2048]{1,0:T(8,128)}), f32[32,2048]{1,0:T(8,128)}) %reduce-scatter.9.cloned.1.call-update) | async-done | bytes 262160 | tf_op jit(solution)/shard_map/reduce_scatter | solution.py:56
  81.4 0.0 copy-done.1
  81.4 1.2 multiply_convert_fusion
  82.7 6.6 %all_gather.14 = bf16[128,2048]{1,0:T(8,128)(2,1)S(1)} all-gather(bf16[32,2048]{1,0:T(8,128)(2,1)S(1)} %get-tuple-element.37), channel_id=1, replica_groups=mesh['dp'=2,'row'=4,'col'=4] {'row'}, dimensions={0}, use_global_device_ids=true | all-gather | bytes 655360 | tf_op jit(solution)/shard_map/all_gather | solution.py:67
  89.3 0.1 convert_reduce_fusion
  89.4 1.3 copy.12
  90.7 0.0 reduce-scatter.19.cloned.1.call-update
  90.7 0.0 reduce-scatter.13.cloned.1.call-start
  90.8 4.5 %fusion.10 = f32[128,1024]{1,0:T(8,128)} fusion(bf16[128,2048]{1,0:T(8,128)(2,1)S(1)} %all_gather.14, bf16[1024,2048]{1,0:T(8,128)(2,1)} %param.11), kind=kOutput, calls=%fused_computation.17 | convolution fusion | flops 536870912 | bytes 5242880 | tf_op jit(solution)/shard_map/dot_general | solution.py:28
  95.3 0.0 reduce-scatter.13.cloned.1.call-update
  95.3 0.0 reduce-scatter.15.cloned.1.call-start
  95.4 4.5 %convolution_bitcast_fusion = f32[1024,2048]{0,1:T(8,128)} fusion(bf16[128,2048]{1,0:T(8,128)(2,1)S(1)} %all_gather.14, bf16[128,1024]{1,0:T(8,128)(2,1)S(1)} %all_gather.13), kind=kOutput, calls=%fused_computation | convolution fusion | flops 536870912 | bytes 9175040 | tf_op jit(solution)/shard_map/dot_general | solution.py:22
  99.9 0.0 reduce-scatter.15.cloned.1.call-update
  99.9 0.0 reduce-scatter.17.cloned.1.call-start
  99.9 7.3 %all_gather.15 = bf16[128,2048]{1,0:T(8,128)(2,1)S(1)} all-gather(bf16[32,2048]{1,0:T(8,128)(2,1)S(1)} %get-tuple-element.36), channel_id=1, replica_groups=mesh['dp'=2,'row'=4,'col'=4] {'row'}, dimensions={0}, use_global_device_ids=true | all-gather | bytes 655360 | tf_op jit(solution)/shard_map/all_gather | solution.py:66
  107.2 4.5 %fusion.11 = f32[2048,1024]{1,0:T(8,128)} fusion(bf16[128,2048]{1,0:T(8,128)(2,1)S(1)} %all_gather.15, bf16[128,1024]{1,0:T(8,128)(2,1)S(1)} %all_gather.12), kind=kOutput, calls=%fused_computation.18 | convolution fusion | flops 536870912 | bytes 9175040 | tf_op jit(solution)/shard_map/dot_general | solution.py:22
  111.7 0.0 reduce-scatter.17.cloned.1.call-update
  111.7 0.1 reduce-scatter.19.cloned.1.call-done
  111.8 1.8 copy.13
  113.6 22.2 %reduce-scatter.13.cloned.1.call-done = f32[32,1024]{1,0:T(8,128)} async-done(((f32[128,1024]{1,0:T(8,128)}), f32[32,1024]{1,0:T(8,128)}) %reduce-scatter.13.cloned.1.call-update) | async-done | bytes 131088 | tf_op jit(solution)/shard_map/reduce_scatter | solution.py:71
  135.8 1.5 convert_element_type.13
  137.4 98.2 %reduce-scatter.15.cloned.1.call-done = f32[1024,1024]{0,1:T(8,128)} async-done(((f32[1024,2048]{0,1:T(8,128)}), f32[1024,1024]{0,1:T(8,128)}) %reduce-scatter.15.cloned.1.call-update) | async-done | bytes 4194320 | tf_op jit(solution)/shard_map/reduce_scatter | solution.py:80
  235.6 11.0 %copy.11 = f32[1024,1,1024]{2,1,0:T(1,128)} copy(f32[1024,1,1024]{0,2,1:T(8,128)} %bitcast.19) | data formatting | bytes 8388608
  246.6 91.1 %reduce-scatter.17.cloned.1.call-done = f32[1024,1024]{1,0:T(8,128)} async-done(((f32[2048,1024]{1,0:T(8,128)}), f32[1024,1024]{1,0:T(8,128)}) %reduce-scatter.17.cloned.1.call-update) | async-done | bytes 4194320 | tf_op jit(solution)/shard_map/reduce_scatter | solution.py:83
  (1 shorter events, 0.0 us)
Async XLA Ops:
  7.2 20.5 %copy-start = (bf16[32,1024]{1,0:T(8,128)(2,1)S(1)}, bf16[32,1024]{1,0:T(8,128)(2,1)}, u32[]{:S(2)}) copy-start(bf16[32,1024]{1,0:T(8,128)(2,1)} %param.14) | copy-start | bytes 196612
  7.2 46.3 %reduce-scatter.11.cloned.1.call-start = ((), (), s32[]{:S(2)}) async-start(), calls=%async_computation.7 | async-start | bytes 1310720 | tf_op jit(solution)/shard_map/reduce_scatter | solution.py:48
  27.0 54.5 %copy-start.1 = (f32[2048]{0:T(1024)S(1)}, f32[2048]{0:T(1024)}, u32[]{:S(2)}) copy-start(f32[2048]{0:T(1024)} %param.12) | copy-start | bytes 24580
  27.0 54.4 %reduce-scatter.9.cloned.1.call-start = ((), (), s32[]{:S(2)}) async-start(), calls=%async_computation.6 | async-start | bytes 1310720 | tf_op jit(solution)/shard_map/reduce_scatter | solution.py:56
  46.9 64.9 %reduce-scatter.19.cloned.1.call-start = ((), (), s32[]{:S(2)}) async-start(), calls=%async_computation.11 | async-start | bytes 1572864
  90.7 45.1 %reduce-scatter.13.cloned.1.call-start = ((), (), s32[]{:S(2)}) async-start(), calls=%async_computation.8 | async-start | bytes 655360 | tf_op jit(solution)/shard_map/reduce_scatter | solution.py:71
  95.3 140.3 %reduce-scatter.15.cloned.1.call-start = ((), (), s32[]{:S(2)}) async-start(), calls=%async_computation.9 | async-start | bytes 12582912 | tf_op jit(solution)/shard_map/reduce_scatter | solution.py:80
  99.9 237.7 %reduce-scatter.17.cloned.1.call-start = ((), (), s32[]{:S(2)}) async-start(), calls=%async_computation.10 | async-start | bytes 12582912 | tf_op jit(solution)/shard_map/reduce_scatter | solution.py:83
Sparse Core Ops, SparseCore 0:
  27.1 26.3 reduce-scatter.10
  56.6 24.8 reduce-scatter.8
  90.8 20.9 reduce-scatter.18
  114.0 21.8 reduce-scatter.12
  138.0 97.5 reduce-scatter.14
  238.3 99.2 reduce-scatter.16
where the time goes:
time: 345 us; the launch traced here: 344 us
  waiting for transfers between devices  246 us (71%)
  blocking collectives  44.2 us (13%)
  matrix products  22 us (6%)
  between operations  14.8 us (4%)
  local copies, waits for them, and re-layouts  14.2 us (4%)
    reduce_scatter x1, waiting for transfers between devices, local(): lax.psum_scatter(up_term, 'dp', scatter_dimension=1, tiled=True)  98.2 us
    reduce_scatter x1, waiting for transfers between devices, local(): lax.psum_scatter(contract_rows(act_all, grads), 'dp', scatter_dimension=0...  91.1 us
    reduce_scatter x1, waiting for transfers between devices, local(): lax.psum_scatter(contract_cols(lax.slice_in_dim(grads, 0, share * lax.axi...  27.9 us
    reduce_scatter x1, waiting for transfers between devices, local(): lax.psum_scatter(contract_cols(lax.slice_in_dim(grad_all, 0, local_rows *...  22.2 us
    all_gather x1, blocking collectives, local(): lax.all_gather(tokens, 'col', axis=0, tiled=True)  15.9 us
    all_gather x1, blocking collectives, local(): lax.all_gather(masked, 'col', axis=0, tiled=True)  14.4 us
    unnamed x7, local copies, waits for them, and re-layouts  14.2 us
    dot_general x2, matrix products, contract_cols(): lax.dot_general(left, right, (((1,), (1,)), ((), ())), preferred_element_...  9.18 us
  transfers between devices with their start and end apart: 6, of which 6 were waited for; matrix products, arithmetic and copies ran while one was open for 9% of the time, Pallas kernels for 0%

commit v1 on v0

v1 whole, which is shorter than its diff:
```python
import functools
import math

import jax
import jax.numpy as jnp
from jax import lax
from jax.experimental import pallas as pl
from jax.experimental.pallas import tpu as pltpu
from jax.sharding import PartitionSpec as P

coef = math.sqrt(2.0 / math.pi)
MESH = pl.DeviceIdType.MESH
BLOCKS = 2


def gelu_pair(pre):
    inner = coef * (pre + 0.044715 * pre * pre * pre)
    tanh_val = jnp.tanh(inner)
    value = 0.5 * pre * (1.0 + tanh_val)
    slope = 0.5 * (1.0 + tanh_val) + 0.5 * pre * (1.0 - tanh_val * tanh_val) * coef * (
        1.0 + 3.0 * 0.044715 * pre * pre
    )
    return (value, slope)


def contract_rows(left, right):
    return lax.dot_general(
        left, right, (((0,), (0,)), ((), ())), preferred_element_type=jnp.float32
    )


def contract_cols(left, right):
    return lax.dot_general(
        left, right, (((1,), (1,)), ((), ())), preferred_element_type=jnp.float32
    )


def flip(index, bits):
    bit = 1
    out = index
    while bit <= bits:
        if bits & bit:
            out = out + bit - 2 * bit * ((index // bit) % 2)
        bit *= 2
    return out


def exchange(
    n_dp, n_row, n_col,
    tok_ref, og_ref, len_ref, bias_ref, wup_hbm, wdn_hbm,
    ig_ref, feats_out, grads_out, act_out, pg_out,
    xg, wup, wdn, part, sent, core_in, mid, row_in, ap, igs, igf, x_in, zs, zr,
    w_sem, own_sem, out_sem, act_sem, ag_send_r, ag_send_l, ag_send_x, ag_recv,
    core_sem, row_sem, pair_sem, igx_send, igx_recv, z_send, z_recv,
):
    dp, row, col = lax.axis_index("dp"), lax.axis_index("row"), lax.axis_index("col")
    bl, width = tok_ref.shape
    blocks = len_ref.shape[0]
    hs = wup.shape[1]
    S = BLOCKS
    nch = n_col // S
    slab = n_dp * bl
    rows = S * slab
    half = rows // 2
    tile = min(256, hs)
    first = pl.multiple_of(dp * hs, hs)
    mate = flip(row, 1)
    mine = row % 2
    far_bits = [1 << b for b in range(1, n_row.bit_length() - 1)]
    pending = []

    w_copies = [
        pltpu.make_async_copy(wup_hbm.at[:, pl.ds(first, hs)], wup, w_sem.at[0]),
        pltpu.make_async_copy(wdn_hbm.at[pl.ds(first, hs), :], wdn, w_sem.at[1]),
    ]
    for copy in w_copies:
        copy.start()

    def group(g):
        return pl.ds(pl.multiple_of(g * bl, bl), bl)

    def block(c, g):
        return xg.at[:, c, group(g), :]

    barrier = pltpu.get_barrier_semaphore()
    peers = [{"dp": (dp + p) % n_dp} for p in range(1, n_dp)]
    peers += [{"col": (col + p) % n_col} for p in range(1, n_col)]
    peers += [{"row": mate}] + [{"row": flip(row, bits)} for bits in far_bits]
    for peer in peers:
        pl.semaphore_signal(barrier, inc=1, device_id=peer, device_id_type=MESH)
    xg[0, col, group(dp), :] = tok_ref[...]
    spot = lax.broadcasted_iota(jnp.int32, (bl, width), 0)
    live = spot < len_ref[0]
    for k in range(1, blocks):
        start = k * (bl // blocks)
        live = jnp.where(spot < start, live, spot - start < len_ref[k])
    out_grad = og_ref[...].astype(jnp.float32)
    xg[1, col, group(dp), :] = jnp.where(live, out_grad, jnp.zeros_like(out_grad)).astype(jnp.bfloat16)
    pl.semaphore_wait(barrier, len(peers))

    def remote(src, dst, send, recv, dev):
        return pltpu.make_async_remote_copy(
            src_ref=src, dst_ref=dst, send_sem=send, recv_sem=recv,
            device_id=dev, device_id_type=MESH,
        )

    def go(copy, cond=None):
        if cond is None:
            copy.start()
        else:
            pl.when(cond)(copy.start)
        pending.append((copy, cond))

    def give(src, c, p):
        return remote(
            src, block(c, dp), ag_send_x.at[p, c], ag_recv.at[dp, c],
            {"dp": (dp + p) % n_dp},
        )

    def send_line(s, src_of):
        low = jnp.maximum(col - s, 0)
        high = jnp.minimum(col + s, n_col - 1)
        if s < n_col - 1:
            right = jnp.minimum(col + 1, n_col - 1)
            left = jnp.maximum(col - 1, 0)
            ok_r = jnp.logical_and(col - s >= 0, col + 1 < n_col)
            ok_l = jnp.logical_and(col + s < n_col, col >= 1)
            go(remote(src_of(low), block(low, dp), ag_send_r.at[s], ag_recv.at[dp, low],
                      {"col": right}), ok_r)
            go(remote(src_of(high), block(high, dp), ag_send_l.at[s], ag_recv.at[dp, high],
                      {"col": left}), ok_l)

    def forward(s):
        low = jnp.maximum(col - s, 0)
        high = jnp.minimum(col + s, n_col - 1)
        for c, cond in ((low, col - s >= 0), (high, col + s < n_col)):
            wait = remote(block(c, dp), block(c, dp), own_sem, ag_recv.at[dp, c], {"col": col})
            pl.when(cond)(wait.wait_recv)
        send_line(s, lambda c: block(c, dp))
        for c, cond in ((low, col - s >= 0), (high, col + s < n_col)):
            for p in range(1, n_dp):
                go(give(block(c, dp), c, p), cond)

    send_line(0, lambda c: block(c, dp))
    for p in range(1, n_dp):
        go(give(block(col, dp), col, p))

    def base(j):
        return S * flip(col // S, j)

    def lanes(n):
        return pl.ds(pl.multiple_of(n * tile, tile), tile)

    def my_half(which):
        return pl.ds(pl.multiple_of(which * half, half), half)

    def stage_a(j):
        for i in range(S):
            c = base(j) + i
            for p in range(1, n_dp):
                g = (dp + p) % n_dp
                remote(block(c, g), block(c, g), own_sem, ag_recv.at[g, c], {"dp": g}).wait_recv()
        if j == 0:
            for copy in w_copies:
                copy.wait()
        b = base(j)

        @pl.loop(0, hs // tile)
        def _(n):
            feats = xg[0, pl.ds(b, S)].reshape(rows, width)
            grads = xg[1, pl.ds(b, S)].reshape(rows, width)
            up = jnp.dot(feats, wup[:, lanes(n)], preferred_element_type=jnp.float32)
            part[j, 0, :, lanes(n)] = up
            sent[j, 0, :, lanes(n)] = up.astype(jnp.bfloat16)
            down = contract_cols(grads, wdn[lanes(n), :])
            part[j, 1, :, lanes(n)] = down
            sent[j, 1, :, lanes(n)] = down.astype(jnp.bfloat16)

        go(remote(sent.at[j, :, my_half(1 - mine), :], core_in.at[j],
                  core_sem.at[0, j], core_sem.at[1, j], {"row": mate}))

    def stage_b(j):
        remote(core_in.at[j], core_in.at[j], own_sem, core_sem.at[1, j], {"row": mate}).wait_recv()

        @pl.loop(0, hs // tile)
        def _(n):
            for k in range(2):
                total = part[j, k, my_half(mine), lanes(n)] + core_in[j, k, :, lanes(n)].astype(jnp.float32)
                mid[j, 0, k, :, lanes(n)] = total.astype(jnp.bfloat16)

        go(remote(mid.at[j, 0], row_in.at[j, 0], row_sem.at[0, j, 0], row_sem.at[1, j, 0],
                  {"row": flip(row, far_bits[0])}))

    def stage_c(j):
        for i, bits in enumerate(far_bits):
            remote(row_in.at[j, i], row_in.at[j, i], own_sem, row_sem.at[1, j, i],
                   {"row": mate}).wait_recv()
            if i + 1 < len(far_bits):
                mid[j, i + 1] = (mid[j, i].astype(jnp.float32) + row_in[j, i].astype(jnp.float32)).astype(jnp.bfloat16)
                go(remote(mid.at[j, i + 1], row_in.at[j, i + 1], row_sem.at[0, j, i + 1],
                          row_sem.at[1, j, i + 1], {"row": flip(row, far_bits[i + 1])}))
        last = len(far_bits) - 1

        @pl.loop(0, hs // tile)
        def _(n):
            pre = mid[j, last, 0, :, lanes(n)].astype(jnp.float32) + row_in[j, last, 0, :, lanes(n)].astype(jnp.float32)
            grad = mid[j, last, 1, :, lanes(n)].astype(jnp.float32) + row_in[j, last, 1, :, lanes(n)].astype(jnp.float32)
            bias = bias_ref[:, pl.ds(pl.multiple_of(dp * hs + n * tile, tile), tile)]
            value, slope = gelu_pair(pre + bias)
            ap[0, j, my_half(mine), lanes(n)] = value.astype(jnp.bfloat16)
            ap[1, j, my_half(mine), lanes(n)] = (grad * slope).astype(jnp.bfloat16)

        here = ap.at[:, j, my_half(mine), :]
        go(remote(here, here, pair_sem.at[0, j], pair_sem.at[1, j], {"row": mate}))

    def stage_d(j):
        there = ap.at[:, j, my_half(1 - mine), :]
        remote(there, there, own_sem, pair_sem.at[1, j], {"row": mate}).wait_recv()

        @pl.loop(0, width // 256)
        def _(n):
            cols = pl.ds(pl.multiple_of(n * 256, 256), 256)
            res = contract_cols(ap[1, j], wup[cols, :])
            igf[j, :, :, cols] = res.reshape(S, slab, 256)
            igs[j, :, :, cols] = res.astype(jnp.bfloat16).reshape(S, slab, 256)

        for p in range(1, n_dp):
            g = (dp + p) % n_dp
            go(remote(igs.at[j, :, group(g), :], x_in.at[j, p], igx_send.at[j, p], igx_recv.at[j, p],
                      {"dp": g}))

    def stage_e(j):
        for p in range(1, n_dp):
            remote(x_in.at[j, p], x_in.at[j, p], own_sem, igx_recv.at[j, p], {"dp": dp}).wait_recv()
        total = igf[j, :, group(dp), :]
        for p in range(1, n_dp):
            total = total + x_in[j, p].astype(jnp.float32)
        zs[j] = total.astype(jnp.bfloat16)
        if j == 0:
            igf[j, :, group(dp), :] = total
        offs = range(1, S) if j == 0 else range(S)
        for i in offs:
            at = (col + i) % S
            c = base(j) + at
            go(remote(zs.at[j, at], zr.at[col], z_send.at[j, i], z_recv.at[col], {"col": c}))

    out_copies = [
        pltpu.make_async_copy(xg.at[0], feats_out, out_sem.at[0]),
        pltpu.make_async_copy(xg.at[1], grads_out, out_sem.at[1]),
    ]
    act_copies = []
    for j in range(nch):
        at = base(j) // S
        act_copies.append(pltpu.make_async_copy(ap.at[0, j], act_out.at[at], act_sem.at[0, j]))
        act_copies.append(pltpu.make_async_copy(ap.at[1, j], pg_out.at[at], act_sem.at[1, j]))

    forward(1)
    if n_col > 2:
        forward(2)
    for t in range(nch + 2):
        if t < nch:
            if t == 1:
                for s in range(3, n_col):
                    forward(s)
            stage_a(t)
            if t == nch - 1:
                for copy in out_copies:
                    copy.start()
        if 0 <= t - 1 < nch:
            if t < nch:
                stage_b(t)
            stage_c(t - 1)
            stage_d(t - 1)
            for copy in act_copies[2 * t - 2 : 2 * t]:
                copy.start()
        elif t < nch:
            stage_b(t)
        if 0 <= t - 2 < nch:
            stage_e(t - 2)
    total = igf[0, col % S, group(dp), :]
    for p in range(1, n_col):
        c = (col + p) % n_col
        remote(zr.at[c], zr.at[c], own_sem, z_recv.at[c], {"col": c}).wait_recv()
        total = total + zr[c].astype(jnp.float32)
    ig_ref[...] = total.astype(jnp.bfloat16)
    for copy, cond in pending:
        if cond is None:
            copy.wait_send()
        else:
            pl.when(cond)(copy.wait_send)
    for copy in out_copies + act_copies:
        copy.wait()


def grads_kernel(feats_ref, pg_ref, act_ref, grads_ref, up_ref, bias_ref, down_ref):
    @pl.when(pl.program_id(0) == 0)
    def _():
        bias_ref[...] = jnp.sum(pg_ref[...].astype(jnp.float32), axis=0, keepdims=True)

    hs = pg_ref.shape[1]
    up = contract_rows(feats_ref[...], pg_ref[...])
    for k in range(hs // 128):
        up_ref[:, k, :] = up[:, k * 128 : (k + 1) * 128]
    down_ref[0] = contract_rows(act_ref[...], grads_ref[...])


def weight_grads(feats, grads, act, pg):
    rows, width = feats.shape
    hs = pg.shape[1]
    steps = max(1, hs // 256)
    f32 = jnp.float32
    return pl.pallas_call(
        grads_kernel,
        grid=(steps,),
        out_shape=(
            jax.ShapeDtypeStruct((width, hs // 128, 128), f32),
            jax.ShapeDtypeStruct((1, hs), f32),
            jax.ShapeDtypeStruct((1, hs, width), f32),
        ),
        in_specs=[
            pl.BlockSpec((rows, width // steps), lambda i: (0, i)),
            pl.BlockSpec((rows, hs), lambda i: (0, 0)),
            pl.BlockSpec((rows, hs // steps), lambda i: (0, i)),
            pl.BlockSpec((rows, width), lambda i: (0, 0)),
        ],
        out_specs=(
            pl.BlockSpec((width // steps, hs // 128, 128), lambda i: (i, 0, 0)),
            pl.BlockSpec((1, hs), lambda i: (0, 0)),
            pl.BlockSpec((1, hs // steps, width), lambda i: (0, i, 0)),
        ),
        compiler_params=pltpu.CompilerParams(vmem_limit_bytes=48 * 1024 * 1024),
    )(feats, pg, act, grads)


def local(n_dp, n_row, n_col, tokens, up_weight, up_bias, down_weight, out_grad, bucket_lengths):
    bl, width = out_grad.shape
    hidden = up_weight.shape[1]
    hs = hidden // n_dp
    S = BLOCKS
    nch = n_col // S
    slab = n_dp * bl
    rows = S * slab
    far = n_row.bit_length() - 2
    bf, f32 = jnp.bfloat16, jnp.float32
    VM, DMA = pltpu.VMEM, pltpu.SemaphoreType.DMA
    vmem = pl.BlockSpec(memory_space=pltpu.VMEM)
    smem = pl.BlockSpec(memory_space=pltpu.SMEM)
    hbm = pl.BlockSpec(memory_space=pl.ANY)
    input_grad, feats, grads, act, pg = pl.pallas_call(
        functools.partial(exchange, n_dp, n_row, n_col),
        out_shape=(
            jax.ShapeDtypeStruct((bl, width), bf),
            jax.ShapeDtypeStruct((n_col, slab, width), bf),
            jax.ShapeDtypeStruct((n_col, slab, width), bf),
            jax.ShapeDtypeStruct((nch, rows, hs), bf),
            jax.ShapeDtypeStruct((nch, rows, hs), bf),
        ),
        in_specs=[vmem, vmem, smem, vmem, hbm, hbm],
        out_specs=(vmem, hbm, hbm, hbm, hbm),
        scratch_shapes=[
            VM((2, n_col, slab, width), bf),
            VM((width, hs), bf),
            VM((hs, width), bf),
            VM((nch, 2, rows, hs), f32),
            VM((nch, 2, rows, hs), bf),
            VM((nch, 2, rows // 2, hs), bf),
            VM((nch, far, 2, rows // 2, hs), bf),
            VM((nch, far, 2, rows // 2, hs), bf),
            VM((2, nch, rows, hs), bf),
            VM((nch, S, slab, width), bf),
            VM((nch, S, slab, width), f32),
            VM((nch, n_dp, S, bl, width), bf),
            VM((nch, S, bl, width), bf),
            VM((n_col, bl, width), bf),
            DMA((2,)), DMA(()), DMA((2,)), DMA((2, nch)),
            DMA((n_col,)), DMA((n_col,)), DMA((n_dp, n_col)), DMA((n_dp, n_col)),
            DMA((2, nch)), DMA((2, nch, far)), DMA((2, nch)),
            DMA((nch, n_dp)), DMA((nch, n_dp)), DMA((nch, S)), DMA((n_col,)),
        ],
        compiler_params=pltpu.CompilerParams(
            collective_id=0, has_side_effects=True, vmem_limit_bytes=60 * 1024 * 1024
        ),
    )(tokens, out_grad, bucket_lengths, up_bias.reshape(1, hidden), up_weight, down_weight)
    feats = feats.reshape(n_col * slab, width)
    grads = grads.reshape(n_col * slab, width)
    act = act.reshape(n_col * slab, hs)
    pg = pg.reshape(n_col * slab, hs)
    up_grad, bias_grad, down_grad = weight_grads(feats, grads, act, pg)
    return (
        input_grad,
        up_grad.reshape(width, 1, hs),
        bias_grad.reshape(1, hs),
        down_grad.reshape(1, hs, width),
    )


def solution(mesh):
    sizes = (mesh.shape["dp"], mesh.shape["row"], mesh.shape["col"])
    return jax.shard_map(
        functools.partial(local, *sizes),
        mesh=mesh,
        in_specs=(
            P(("dp", "col"), "row"),
            P("row", "col"),
            P("col"),
            P("col", "row"),
            P(("dp", "col"), "row"),
            P(("dp", "col")),
        ),
        out_specs=(
            P(("dp", "col"), "row"),
            P("row", "col", "dp"),
            P("col", "dp"),
            P("col", "dp", "row"),
        ),
        check_vma=False,
    )
```

time: 345 us -> 59.6 us (0.17)
  waiting for transfers between devices: 246 us -> 0 us
  Pallas kernels: 0 us -> 52.2 us
  blocking collectives: 44.2 us -> 0 us
  matrix products: 22 us -> 0 us
  between operations: 14.8 us -> 1.3 us
  local copies, waits for them, and re-layouts: 14.2 us -> 5.63 us
    reduce_scatter x5 -> x0, waiting for transfers between devices: 246 us -> none  [the longest x1 98.2 us: local(): lax.psum_scatter(up_term, 'dp', scatter_dimension=1, tiled=True)]
    pallas_call x0 -> x2, Pallas kernels: none -> 52.2 us  [the longest x1 46.7 us: local(): pl.pallas_call(functools.partial(exchange, n_dp, n_row, n_col), out_shape...]
    all_gather x4 -> x0, blocking collectives: 44.2 us -> none  [the longest x1 15.9 us: local(): lax.all_gather(tokens, 'col', axis=0, tiled=True)]
    dot_general x5 -> x0, matrix products: 22 us -> none  [the longest x2 9.18 us: contract_cols(): lax.dot_general(left, right, (((1,), (1,)), ((), ())), preferred_element_...]
    unnamed x7 -> x9, local copies, waits for them, and re-layouts: 14.2 us -> 5.63 us
  transfers between devices with their start and end apart: 6 -> 0, of which waited for: 6 -> 0; matrix products, arithmetic and copies ran while one was open for 9% -> 0% of each run, Pallas kernels for 0% -> 0%
where the time goes in v1:
time: 59.6 us; the launch traced here: 59.2 us
  Pallas kernels  52.2 us (88%)
  local copies, waits for them, and re-layouts  5.63 us (9%)
  between operations  1.3 us (2%)
    pallas_call x1, Pallas kernels, local(): pl.pallas_call(functools.partial(exchange, n_dp, n_row, n_col), out_shape...  46.7 us
    unnamed x9, local copies, waits for them, and re-layouts  5.63 us
    pallas_call x1, Pallas kernels, weight_grads(): pl.pallas_call(grads_kernel, grid=(steps,), out_shape=(jax.ShapeDtypeStru...  5.49 us

profile of v1, /device:TPU:0, one launch (start us, length us, event | category | flops | bytes accessed | tf_op | source)
XLA Modules:
  0.0 59.2 jit_solution(476585809953987502)
XLA Ops:
  1.3 46.7 %shard_map.93 = (bf16[32,1024]{1,0:T(8,128)(2,1)}, bf16[4,64,1024]{2,1,0:T(8,128)(2,1)}, bf16[4,64,1024]{2,1,0:T(8,128)(2,1)}, bf16[2,128,1024]{2,1,0:T(8,128)(2,1)}, bf16[2,128,1024]{2,1,0:T(8,128)(2,1)}) custom-call(bf16[32,1024]{1,0:T(8,128)(2,1)} %tok_ref.1, bf16[32,1024]{1,0:T(8,128)(2,1)} %og_ref.1, s32[1]{0:T(128)S(6)} %copy.12.len_ref, ...), custom_call_target="tpu_custom_call" | custom-call | tf_op jit(solution)/shard_map/pallas_call | solution.py:349
  48.0 0.0 copy-start
  48.0 1.0 %copy-done = bf16[4,64,1024]{2,1,0:T(8,128)(2,1)S(1)} copy-done((bf16[4,64,1024]{2,1,0:T(8,128)(2,1)S(1)}, bf16[4,64,1024]{2,1,0:T(8,128)(2,1)}, u32[]{:S(2)}) %copy-start) | copy-done | bytes 524312
  49.1 0.0 copy-start.1
  49.1 1.0 %copy-done.1 = bf16[4,64,1024]{2,1,0:T(8,128)(2,1)S(1)} copy-done((bf16[4,64,1024]{2,1,0:T(8,128)(2,1)S(1)}, bf16[4,64,1024]{2,1,0:T(8,128)(2,1)}, u32[]{:S(2)}) %copy-start.1) | copy-done | bytes 524312
  50.1 0.0 copy-start.2
  50.1 1.0 %copy-done.2 = bf16[2,128,1024]{2,1,0:T(8,128)(2,1)S(1)} copy-done((bf16[2,128,1024]{2,1,0:T(8,128)(2,1)S(1)}, bf16[2,128,1024]{2,1,0:T(8,128)(2,1)}, u32[]{:S(2)}) %copy-start.2) | copy-done | bytes 524312
  51.2 0.0 copy-start.3
  51.2 1.0 %copy-done.3 = bf16[2,128,1024]{2,1,0:T(8,128)(2,1)S(1)} copy-done((bf16[2,128,1024]{2,1,0:T(8,128)(2,1)S(1)}, bf16[2,128,1024]{2,1,0:T(8,128)(2,1)}, u32[]{:S(2)}) %copy-start.3) | copy-done | bytes 524312
  52.2 5.5 %shard_map.94 = (f32[1024,8,128]{2,1,0:T(8,128)}, f32[1,1024]{1,0:T(1,128)}, f32[1,1024,1024]{2,1,0:T(8,128)}) custom-call(bf16[256,1024]{1,0:T(8,128)(2,1)S(1)} %bitcast.6, bf16[256,1024]{1,0:T(8,128)(2,1)S(1)} %bitcast.9, bf16[256,1024]{1,0:T(8,128)(2,1)S(1)} %bitcast.8, bf16[256,1024]{1,0:T(8,128)(2,1)S(1)} %bitcast.7), custom_call_target="tpu_custom_call" | custom-call | tf_op jit(solution)/shard_map/pallas_call | solution.py:312
  57.7 1.5 %copy.13 = bf16[32,1024]{1,0:T(8,128)(2,1)} copy(bf16[32,1024]{1,0:T(8,128)(2,1)} %get-tuple-element.28) | data formatting | bytes 131072
Async XLA Ops:
  48.0 1.0 %copy-start = (bf16[4,64,1024]{2,1,0:T(8,128)(2,1)S(1)}, bf16[4,64,1024]{2,1,0:T(8,128)(2,1)}, u32[]{:S(2)}) copy-start(bf16[4,64,1024]{2,1,0:T(8,128)(2,1)} %get-tuple-element.13) | copy-start | bytes 1572868
  49.1 1.0 %copy-start.1 = (bf16[4,64,1024]{2,1,0:T(8,128)(2,1)S(1)}, bf16[4,64,1024]{2,1,0:T(8,128)(2,1)}, u32[]{:S(2)}) copy-start(bf16[4,64,1024]{2,1,0:T(8,128)(2,1)} %get-tuple-element.16) | copy-start | bytes 1572868
  50.1 1.0 %copy-start.2 = (bf16[2,128,1024]{2,1,0:T(8,128)(2,1)S(1)}, bf16[2,128,1024]{2,1,0:T(8,128)(2,1)}, u32[]{:S(2)}) copy-start(bf16[2,128,1024]{2,1,0:T(8,128)(2,1)} %get-tuple-element.15) | copy-start | bytes 1572868
  51.2 1.0 %copy-start.3 = (bf16[2,128,1024]{2,1,0:T(8,128)(2,1)S(1)}, bf16[2,128,1024]{2,1,0:T(8,128)(2,1)}, u32[]{:S(2)}) copy-start(bf16[2,128,1024]{2,1,0:T(8,128)(2,1)} %get-tuple-element.14) | copy-start | bytes 1572868

commit v2 on v1

--- a/solution.py
+++ b/solution.py
@@ -79,15 +79,20 @@
     def group(g):
         return pl.ds(pl.multiple_of(g * bl, bl), bl)
 
-    def block(c, g):
-        return xg.at[:, c, group(g), :]
+    def block(k, c, g):
+        return xg.at[k, c, group(g), :]
 
     barrier = pltpu.get_barrier_semaphore()
     peers = [{"dp": (dp + p) % n_dp} for p in range(1, n_dp)]
-    peers += [{"col": (col + p) % n_col} for p in range(1, n_col)]
     peers += [{"row": mate}] + [{"row": flip(row, bits)} for bits in far_bits]
     for peer in peers:
         pl.semaphore_signal(barrier, inc=1, device_id=peer, device_id_type=MESH)
+    has_r, has_l = col + 1 < n_col, col >= 1
+    step_r, step_l = jnp.minimum(col + 1, n_col - 1), jnp.maximum(col - 1, 0)
+    for cond, c in ((has_r, step_r), (has_l, step_l)):
+        @pl.when(cond)
+        def _():
+            pl.semaphore_signal(barrier, inc=1, device_id={"col": c}, device_id_type=MESH)
     xg[0, col, group(dp), :] = tok_ref[...]
     spot = lax.broadcasted_iota(jnp.int32, (bl, width), 0)
     live = spot < len_ref[0]
@@ -96,7 +101,8 @@
         live = jnp.where(spot < start, live, spot - start < len_ref[k])
     out_grad = og_ref[...].astype(jnp.float32)
     xg[1, col, group(dp), :] = jnp.where(live, out_grad, jnp.zeros_like(out_grad)).astype(jnp.bfloat16)
-    pl.semaphore_wait(barrier, len(peers))
+    beside = jnp.minimum(n_col - 1 - col, 1) + jnp.minimum(col, 1)
+    pl.semaphore_wait(barrier, len(peers) + beside)
 
     def remote(src, dst, send, recv, dev):
         return pltpu.make_async_remote_copy(
@@ -111,39 +117,38 @@
             pl.when(cond)(copy.start)
         pending.append((copy, cond))
 
-    def give(src, c, p):
+    def give(k, c, p):
         return remote(
-            src, block(c, dp), ag_send_x.at[p, c], ag_recv.at[dp, c],
+            block(k, c, dp), block(k, c, dp), ag_send_x.at[k, p, c], ag_recv.at[k, dp, c],
             {"dp": (dp + p) % n_dp},
         )
 
-    def send_line(s, src_of):
-        low = jnp.maximum(col - s, 0)
-        high = jnp.minimum(col + s, n_col - 1)
-        if s < n_col - 1:
-            right = jnp.minimum(col + 1, n_col - 1)
-            left = jnp.maximum(col - 1, 0)
-            ok_r = jnp.logical_and(col - s >= 0, col + 1 < n_col)
-            ok_l = jnp.logical_and(col + s < n_col, col >= 1)
-            go(remote(src_of(low), block(low, dp), ag_send_r.at[s], ag_recv.at[dp, low],
-                      {"col": right}), ok_r)
-            go(remote(src_of(high), block(high, dp), ag_send_l.at[s], ag_recv.at[dp, high],
-                      {"col": left}), ok_l)
+    def arrived(k, c, g):
+        return remote(block(k, c, g), block(k, c, g), own_sem, ag_recv.at[k, g, c], {"col": col})
 
     def forward(s):
         low = jnp.maximum(col - s, 0)
         high = jnp.minimum(col + s, n_col - 1)
-        for c, cond in ((low, col - s >= 0), (high, col + s < n_col)):
-            wait = remote(block(c, dp), block(c, dp), own_sem, ag_recv.at[dp, c], {"col": col})
-            pl.when(cond)(wait.wait_recv)
-        send_line(s, lambda c: block(c, dp))
-        for c, cond in ((low, col - s >= 0), (high, col + s < n_col)):
-            for p in range(1, n_dp):
-                go(give(block(c, dp), c, p), cond)
-
-    send_line(0, lambda c: block(c, dp))
-    for p in range(1, n_dp):
-        go(give(block(col, dp), col, p))
+        has_low, has_high = col - s >= 0, col + s < n_col
+        for k in range(2):
+            for c, cond, edge, to, sems in (
+                (low, has_low, has_r, step_r, ag_send_r),
+                (high, has_high, has_l, step_l, ag_send_l),
+            ):
+                if s > 0:
+                    pl.when(cond)(arrived(k, c, dp).wait_recv)
+                if s < n_col - 1:
+                    go(remote(block(k, c, dp), block(k, c, dp), sems.at[k, s],
+                              ag_recv.at[k, dp, c], {"col": to}), jnp.logical_and(cond, edge))
+            if s == 0:
+                for p in range(1, n_dp):
+                    go(give(k, col, p))
+            else:
+                for c, cond in ((low, has_low), (high, has_high)):
+                    for p in range(1, n_dp):
+                        go(give(k, c, p), cond)
+
+    forward(0)
 
     def base(j):
         return S * flip(col // S, j)
@@ -159,7 +164,8 @@
             c = base(j) + i
             for p in range(1, n_dp):
                 g = (dp + p) % n_dp
-                remote(block(c, g), block(c, g), own_sem, ag_recv.at[g, c], {"dp": g}).wait_recv()
+                for k in range(2):
+                    arrived(k, c, g).wait_recv()
         if j == 0:
             for copy in w_copies:
                 copy.wait()
@@ -213,36 +219,37 @@
         here = ap.at[:, j, my_half(mine), :]
         go(remote(here, here, pair_sem.at[0, j], pair_sem.at[1, j], {"row": mate}))
 
-    def stage_d(j):
-        there = ap.at[:, j, my_half(1 - mine), :]
-        remote(there, there, own_sem, pair_sem.at[1, j], {"row": mate}).wait_recv()
-
-        @pl.loop(0, width // 256)
+    def stage_d(j, other):
+        i = 1 - mine if other else mine
+        if other:
+            there = ap.at[:, j, my_half(i), :]
+            remote(there, there, own_sem, pair_sem.at[1, j], {"row": mate}).wait_recv()
+        wide = min(512, width)
+
+        @pl.loop(0, width // wide)
         def _(n):
-            cols = pl.ds(pl.multiple_of(n * 256, 256), 256)
-            res = contract_cols(ap[1, j], wup[cols, :])
-            igf[j, :, :, cols] = res.reshape(S, slab, 256)
-            igs[j, :, :, cols] = res.astype(jnp.bfloat16).reshape(S, slab, 256)
+            cols = pl.ds(pl.multiple_of(n * wide, wide), wide)
+            res = contract_cols(ap[1, j, my_half(i), :], wup[cols, :])
+            igf[j, i, :, cols] = res
+            igs[j, i, :, cols] = res.astype(jnp.bfloat16)
 
         for p in range(1, n_dp):
             g = (dp + p) % n_dp
-            go(remote(igs.at[j, :, group(g), :], x_in.at[j, p], igx_send.at[j, p], igx_recv.at[j, p],
-                      {"dp": g}))
-
-    def stage_e(j):
+            go(remote(igs.at[j, i, group(g), :], x_in.at[j, p, i], igx_send.at[j, p, i],
+                      igx_recv.at[j, p, i], {"dp": g}))
+
+    def stage_e(j, other):
+        i = 1 - mine if other else mine
         for p in range(1, n_dp):
-            remote(x_in.at[j, p], x_in.at[j, p], own_sem, igx_recv.at[j, p], {"dp": dp}).wait_recv()
-        total = igf[j, :, group(dp), :]
+            remote(x_in.at[j, p, i], x_in.at[j, p, i], own_sem, igx_recv.at[j, p, i], {"dp": dp}).wait_recv()
+        total = igf[j, i, group(dp), :]
         for p in range(1, n_dp):
-            total = total + x_in[j, p].astype(jnp.float32)
-        zs[j] = total.astype(jnp.bfloat16)
+            total = total + x_in[j, p, i].astype(jnp.float32)
+        zs[j, i] = total.astype(jnp.bfloat16)
         if j == 0:
-            igf[j, :, group(dp), :] = total
-        offs = range(1, S) if j == 0 else range(S)
-        for i in offs:
-            at = (col + i) % S
-            c = base(j) + at
-            go(remote(zs.at[j, at], zr.at[col], z_send.at[j, i], z_recv.at[col], {"col": c}))
+            igf[j, i, group(dp), :] = total
+        cond = i != col % S if j == 0 else None
+        go(remote(zs.at[j, i], zr.at[col], z_send.at[j, i], z_recv.at[col], {"col": base(j) + i}), cond)
 
     out_copies = [
         pltpu.make_async_copy(xg.at[0], feats_out, out_sem.at[0]),
@@ -254,29 +261,28 @@
         act_copies.append(pltpu.make_async_copy(ap.at[0, j], act_out.at[at], act_sem.at[0, j]))
         act_copies.append(pltpu.make_async_copy(ap.at[1, j], pg_out.at[at], act_sem.at[1, j]))
 
-    forward(1)
-    if n_col > 2:
-        forward(2)
-    for t in range(nch + 2):
-        if t < nch:
-            if t == 1:
-                for s in range(3, n_col):
-                    forward(s)
-            stage_a(t)
-            if t == nch - 1:
-                for copy in out_copies:
-                    copy.start()
-        if 0 <= t - 1 < nch:
-            if t < nch:
-                stage_b(t)
-            stage_c(t - 1)
-            stage_d(t - 1)
-            for copy in act_copies[2 * t - 2 : 2 * t]:
-                copy.start()
-        elif t < nch:
-            stage_b(t)
-        if 0 <= t - 2 < nch:
-            stage_e(t - 2)
+    def finish(copies):
+        for copy in copies:
+            copy.start()
+
+    steps = [(forward, s) for s in range(1, min(S + 1, n_col))]
+    steps += [(stage_a, 0), (stage_b, 0)]
+    for t in range(1, nch):
+        if t == 1:
+            steps += [(forward, s) for s in range(S + 1, n_col)]
+        steps += [(stage_a, t)]
+        if t == nch - 1:
+            steps += [(finish, out_copies)]
+        steps += [(stage_c, t - 1), (stage_b, t), (stage_d, t - 1, 0), (stage_d, t - 1, 1)]
+        steps += [(finish, act_copies[2 * t - 2 : 2 * t])]
+        steps += [(stage_e, t - 1, 0), (stage_e, t - 1, 1)]
+    if nch == 1:
+        steps += [(finish, out_copies)]
+    t = nch - 1
+    steps += [(stage_c, t), (stage_d, t, 0), (stage_d, t, 1), (finish, act_copies[2 * t :])]
+    steps += [(stage_e, t, 0), (stage_e, t, 1)]
+    for step, *args in steps:
+        step(*args)
     total = igf[0, col % S, group(dp), :]
     for p in range(1, n_col):
         c = (col + p) % n_col
@@ -292,10 +298,11 @@
         copy.wait()
 
 
-def grads_kernel(feats_ref, pg_ref, act_ref, grads_ref, up_ref, bias_ref, down_ref):
+def grads_kernel(feats_ref, pg_ref, act_ref, grads_ref, ig_ref, up_ref, bias_ref, down_ref, out_ref):
     @pl.when(pl.program_id(0) == 0)
     def _():
         bias_ref[...] = jnp.sum(pg_ref[...].astype(jnp.float32), axis=0, keepdims=True)
+        out_ref[...] = ig_ref[...]
 
     hs = pg_ref.shape[1]
     up = contract_rows(feats_ref[...], pg_ref[...])
@@ -304,7 +311,7 @@
     down_ref[0] = contract_rows(act_ref[...], grads_ref[...])
 
 
-def weight_grads(feats, grads, act, pg):
+def weight_grads(feats, grads, act, pg, input_grad):
     rows, width = feats.shape
     hs = pg.shape[1]
     steps = max(1, hs // 256)
@@ -316,20 +323,23 @@
             jax.ShapeDtypeStruct((width, hs // 128, 128), f32),
             jax.ShapeDtypeStruct((1, hs), f32),
             jax.ShapeDtypeStruct((1, hs, width), f32),
+            jax.ShapeDtypeStruct(input_grad.shape, input_grad.dtype),
         ),
         in_specs=[
             pl.BlockSpec((rows, width // steps), lambda i: (0, i)),
-            pl.BlockSpec((rows, hs), lambda i: (0, 0)),
+            pl.BlockSpec((rows, hs), lambda i: (0, 0), pipeline_mode=pl.Buffered(1)),
             pl.BlockSpec((rows, hs // steps), lambda i: (0, i)),
-            pl.BlockSpec((rows, width), lambda i: (0, 0)),
+            pl.BlockSpec((rows, width), lambda i: (0, 0), pipeline_mode=pl.Buffered(1)),
+            pl.BlockSpec(input_grad.shape, lambda i: (0, 0), pipeline_mode=pl.Buffered(1)),
         ],
         out_specs=(
             pl.BlockSpec((width // steps, hs // 128, 128), lambda i: (i, 0, 0)),
             pl.BlockSpec((1, hs), lambda i: (0, 0)),
             pl.BlockSpec((1, hs // steps, width), lambda i: (0, i, 0)),
-        ),
-        compiler_params=pltpu.CompilerParams(vmem_limit_bytes=48 * 1024 * 1024),
-    )(feats, pg, act, grads)
+            pl.BlockSpec(input_grad.shape, lambda i: (0, 0)),
+        ),
+        compiler_params=pltpu.CompilerParams(vmem_limit_bytes=63 * 1024 * 1024),
+    )(feats, pg, act, grads, input_grad)
 
 
 def local(n_dp, n_row, n_col, tokens, up_weight, up_bias, down_weight, out_grad, bucket_lengths):
@@ -373,9 +383,9 @@
             VM((nch, S, bl, width), bf),
             VM((n_col, bl, width), bf),
             DMA((2,)), DMA(()), DMA((2,)), DMA((2, nch)),
-            DMA((n_col,)), DMA((n_col,)), DMA((n_dp, n_col)), DMA((n_dp, n_col)),
+            DMA((2, n_col)), DMA((2, n_col)), DMA((2, n_dp, n_col)), DMA((2, n_dp, n_col)),
             DMA((2, nch)), DMA((2, nch, far)), DMA((2, nch)),
-            DMA((nch, n_dp)), DMA((nch, n_dp)), DMA((nch, S)), DMA((n_col,)),
+            DMA((nch, n_dp, S)), DMA((nch, n_dp, S)), DMA((nch, S)), DMA((n_col,)),
         ],
         compiler_params=pltpu.CompilerParams(
             collective_id=0, has_side_effects=True, vmem_limit_bytes=60 * 1024 * 1024
@@ -385,7 +395,7 @@
     grads = grads.reshape(n_col * slab, width)
     act = act.reshape(n_col * slab, hs)
     pg = pg.reshape(n_col * slab, hs)
-    up_grad, bias_grad, down_grad = weight_grads(feats, grads, act, pg)
+    up_grad, bias_grad, down_grad, input_grad = weight_grads(feats, grads, act, pg, input_grad)
     return (
         input_grad,
         up_grad.reshape(width, 1, hs),

time: 59.6 us -> 54.2 us (0.909)
  local copies, waits for them, and re-layouts: 5.63 us -> 0 us
    unnamed x9 -> x0, local copies, waits for them, and re-layouts: 5.63 us -> none
    pallas_call x1, Pallas kernels: 5.49 us -> 7.17 us  [weight_grads(): pl.pallas_call(grads_kernel, grid=(steps,), out_shape=(jax.ShapeDtypeStru...]
    pallas_call x1, Pallas kernels: 46.7 us -> 45.2 us  [local(): pl.pallas_call(functools.partial(exchange, n_dp, n_row, n_col), out_shape...]
where the time goes in v2:
time: 54.2 us; the launch traced here: 53.6 us
  Pallas kernels  52.3 us (96%)
  between operations  1.29 us (2%)
    pallas_call x1, Pallas kernels, local(): pl.pallas_call(functools.partial(exchange, n_dp, n_row, n_col), out_shape...  45.2 us
    pallas_call x1, Pallas kernels, weight_grads(): pl.pallas_call(grads_kernel, grid=(steps,), out_shape=(jax.ShapeDtypeStru...  7.17 us

profile of v2, /device:TPU:0, one launch (start us, length us, event | category | flops | bytes accessed | tf_op | source)
XLA Modules:
  0.0 53.6 jit_solution(1985464543085547905)
XLA Ops:
  1.3 45.2 %shard_map.93 = (bf16[32,1024]{1,0:T(8,128)(2,1)}, bf16[4,64,1024]{2,1,0:T(8,128)(2,1)}, bf16[4,64,1024]{2,1,0:T(8,128)(2,1)}, bf16[2,128,1024]{2,1,0:T(8,128)(2,1)}, bf16[2,128,1024]{2,1,0:T(8,128)(2,1)}) custom-call(bf16[32,1024]{1,0:T(8,128)(2,1)} %tok_ref.1, bf16[32,1024]{1,0:T(8,128)(2,1)} %og_ref.1, s32[1]{0:T(128)S(6)} %copy.11.len_ref, ...), custom_call_target="tpu_custom_call" | custom-call | tf_op jit(solution)/shard_map/pallas_call | solution.py:359
  46.5 7.2 %shard_map.94 = (f32[1024,8,128]{2,1,0:T(8,128)}, f32[1,1024]{1,0:T(1,128)}, f32[1,1024,1024]{2,1,0:T(8,128)}, bf16[32,1024]{1,0:T(8,128)(2,1)}) custom-call(bf16[256,1024]{1,0:T(8,128)(2,1)} %bitcast.6, bf16[256,1024]{1,0:T(8,128)(2,1)} %bitcast.9, bf16[256,1024]{1,0:T(8,128)(2,1)} %bitcast.8, bf16[256,1024]{1,0:T(8,128)(2,1)} %bitcast.7, ...), custom_call_target="tpu_custom_call" | custom-call | tf_op jit(solution)/shard_map/pallas_call | solution.py:319

commit v3 on v2

--- a/solution.py
+++ b/solution.py
@@ -10,7 +10,7 @@
 
 coef = math.sqrt(2.0 / math.pi)
 MESH = pl.DeviceIdType.MESH
-BLOCKS = 2
+BLOCKS = 1
 
 
 def gelu_pair(pre):
@@ -219,37 +219,38 @@
         here = ap.at[:, j, my_half(mine), :]
         go(remote(here, here, pair_sem.at[0, j], pair_sem.at[1, j], {"row": mate}))
 
-    def stage_d(j, other):
-        i = 1 - mine if other else mine
-        if other:
-            there = ap.at[:, j, my_half(i), :]
-            remote(there, there, own_sem, pair_sem.at[1, j], {"row": mate}).wait_recv()
-        wide = min(512, width)
+    def stage_d(j):
+        there = ap.at[:, j, my_half(1 - mine), :]
+        remote(there, there, own_sem, pair_sem.at[1, j], {"row": mate}).wait_recv()
+        wide = min(256, width)
 
         @pl.loop(0, width // wide)
         def _(n):
             cols = pl.ds(pl.multiple_of(n * wide, wide), wide)
-            res = contract_cols(ap[1, j, my_half(i), :], wup[cols, :])
-            igf[j, i, :, cols] = res
-            igs[j, i, :, cols] = res.astype(jnp.bfloat16)
-
-        for p in range(1, n_dp):
-            g = (dp + p) % n_dp
-            go(remote(igs.at[j, i, group(g), :], x_in.at[j, p, i], igx_send.at[j, p, i],
-                      igx_recv.at[j, p, i], {"dp": g}))
-
-    def stage_e(j, other):
-        i = 1 - mine if other else mine
-        for p in range(1, n_dp):
-            remote(x_in.at[j, p, i], x_in.at[j, p, i], own_sem, igx_recv.at[j, p, i], {"dp": dp}).wait_recv()
-        total = igf[j, i, group(dp), :]
-        for p in range(1, n_dp):
-            total = total + x_in[j, p, i].astype(jnp.float32)
-        zs[j, i] = total.astype(jnp.bfloat16)
-        if j == 0:
-            igf[j, i, group(dp), :] = total
-        cond = i != col % S if j == 0 else None
-        go(remote(zs.at[j, i], zr.at[col], z_send.at[j, i], z_recv.at[col], {"col": base(j) + i}), cond)
+            res = contract_cols(ap[1, j], wup[cols, :])
+            for i in range(S):
+                igf[j, i, :, cols] = res[i * slab : (i + 1) * slab]
+                igs[j, i, :, cols] = res[i * slab : (i + 1) * slab].astype(jnp.bfloat16)
+
+        for i in range(S):
+            for p in range(1, n_dp):
+                g = (dp + p) % n_dp
+                go(remote(igs.at[j, i, group(g), :], x_in.at[j, p, i], igx_send.at[j, p, i],
+                          igx_recv.at[j, p, i], {"dp": g}))
+
+    def stage_e(j):
+        for i in range(S):
+            for p in range(1, n_dp):
+                remote(x_in.at[j, p, i], x_in.at[j, p, i], own_sem, igx_recv.at[j, p, i], {"dp": dp}).wait_recv()
+            total = igf[j, i, group(dp), :]
+            for p in range(1, n_dp):
+                total = total + x_in[j, p, i].astype(jnp.float32)
+            if j == 0:
+                igf[j, i, group(dp), :] = total
+            if j > 0 or S > 1:
+                zs[j, i] = total.astype(jnp.bfloat16)
+                cond = i != col % S if j == 0 else None
+                go(remote(zs.at[j, i], zr.at[col], z_send.at[j, i], z_recv.at[col], {"col": base(j) + i}), cond)
 
     out_copies = [
         pltpu.make_async_copy(xg.at[0], feats_out, out_sem.at[0]),
@@ -266,21 +267,25 @@
             copy.start()
 
     steps = [(forward, s) for s in range(1, min(S + 1, n_col))]
-    steps += [(stage_a, 0), (stage_b, 0)]
-    for t in range(1, nch):
-        if t == 1:
-            steps += [(forward, s) for s in range(S + 1, n_col)]
-        steps += [(stage_a, t)]
-        if t == nch - 1:
-            steps += [(finish, out_copies)]
-        steps += [(stage_c, t - 1), (stage_b, t), (stage_d, t - 1, 0), (stage_d, t - 1, 1)]
-        steps += [(finish, act_copies[2 * t - 2 : 2 * t])]
-        steps += [(stage_e, t - 1, 0), (stage_e, t - 1, 1)]
-    if nch == 1:
-        steps += [(finish, out_copies)]
-    t = nch - 1
-    steps += [(stage_c, t), (stage_d, t, 0), (stage_d, t, 1), (finish, act_copies[2 * t :])]
-    steps += [(stage_e, t, 0), (stage_e, t, 1)]
+    waits = [(forward, s) for s in range(S + 1, n_col)]
+    for t in range(nch + 2):
+        if t < nch:
+            if t == nch - 1:
+                steps += waits
+                waits = []
+            steps += [(stage_a, t)]
+            steps += waits[:1]
+            waits = waits[1:]
+            if t == nch - 1:
+                steps += [(finish, out_copies)]
+        if 0 <= t - 1 < nch:
+            steps += [(stage_c, t - 1)]
+        if t < nch:
+            steps += [(stage_b, t)]
+        if 0 <= t - 1 < nch:
+            steps += [(stage_d, t - 1), (finish, act_copies[2 * t - 2 : 2 * t])]
+        if 0 <= t - 2 < nch:
+            steps += [(stage_e, t - 2)]
     for step, *args in steps:
         step(*args)
     total = igf[0, col % S, group(dp), :]
@@ -314,7 +319,7 @@
 def weight_grads(feats, grads, act, pg, input_grad):
     rows, width = feats.shape
     hs = pg.shape[1]
-    steps = max(1, hs // 256)
+    steps = max(1, hs // 512)
     f32 = jnp.float32
     return pl.pallas_call(
         grads_kernel,

time: 54.2 us -> 52 us (0.959)
  Pallas kernels: 52.3 us -> 50.5 us
    pallas_call x1, Pallas kernels: 45.2 us -> 43.8 us  [local(): pl.pallas_call(functools.partial(exchange, n_dp, n_row, n_col), out_shape...]
where the time goes in v3:
time: 52 us; the launch traced here: 51.8 us
  Pallas kernels  50.5 us (97%)
  between operations  1.29 us (2%)
    pallas_call x1, Pallas kernels, local(): pl.pallas_call(functools.partial(exchange, n_dp, n_row, n_col), out_shape...  43.8 us
    pallas_call x1, Pallas kernels, weight_grads(): pl.pallas_call(grads_kernel, grid=(steps,), out_shape=(jax.ShapeDtypeStru...  6.71 us

profile of v3, /device:TPU:0, one launch (start us, length us, event | category | flops | bytes accessed | tf_op | source)
XLA Modules:
  0.0 51.8 jit_solution(7152997352596398146)
XLA Ops:
  1.3 43.8 %shard_map.93 = (bf16[32,1024]{1,0:T(8,128)(2,1)}, bf16[4,64,1024]{2,1,0:T(8,128)(2,1)}, bf16[4,64,1024]{2,1,0:T(8,128)(2,1)}, bf16[4,64,1024]{2,1,0:T(8,128)(2,1)}, bf16[4,64,1024]{2,1,0:T(8,128)(2,1)}) custom-call(bf16[32,1024]{1,0:T(8,128)(2,1)} %tok_ref.1, bf16[32,1024]{1,0:T(8,128)(2,1)} %og_ref.1, s32[1]{0:T(128)S(6)} %copy.11.len_ref, ...), custom_call_target="tpu_custom_call" | custom-call | tf_op jit(solution)/shard_map/pallas_call | solution.py:364
  45.1 6.7 %shard_map.94 = (f32[1024,8,128]{2,1,0:T(8,128)}, f32[1,1024]{1,0:T(1,128)}, f32[1,1024,1024]{2,1,0:T(8,128)}, bf16[32,1024]{1,0:T(8,128)(2,1)}) custom-call(bf16[256,1024]{1,0:T(8,128)(2,1)} %bitcast.6, bf16[256,1024]{1,0:T(8,128)(2,1)} %bitcast.9, bf16[256,1024]{1,0:T(8,128)(2,1)} %bitcast.8, bf16[256,1024]{1,0:T(8,128)(2,1)} %bitcast.7, ...), custom_call_target="tpu_custom_call" | custom-call | tf_op jit(solution)/shard_map/pallas_call | solution.py:324
